TPU v7x, 32 devices: a whole 2x2x4 slice. The times are simulated.
32 devices in a mesh: dp: 2 (over y), ctx: 8 (over z, x), segment: 2 (over core).
Axes of the slice: x: 2, y: 2, z: 4, core: 2. Of those that a mesh axis runs over, the one named last changes fastest.
Arguments:
- inputs: bfloat16 [2, 2048, 1536], P('dp', 'ctx'), may hold values from -6 to 6
- cotangent: bfloat16 [2, 2048, 1536], P('dp', 'ctx'), may hold values from -6 to 6
- weights: bfloat16 [2, 1536, 1536], P('segment', 'ctx'), may hold values from -0.15625 to 0.15625
- tap_weights: float32 [2, 3, 1536], P('segment'), may hold values from -3 to 3
- projection: bfloat16 [2, 1536, 256], P('segment'), may hold values from -0.15625 to 0.15625
- dilations: int32 [2], replicated, may hold values from 1 to 64, as said below
Outputs:
- input_grad: bfloat16 [2, 2048, 1536], P('dp', 'ctx', 'segment')
- sketches: float32 [2, 256, 1536], P('segment', 'ctx')
Inputs may be any that keep to these rules, and one draw needn't show every extreme that they name: `dilations`: each entry is a section's dilation; one of the two equals 64.
All inputs are finite; a program needn't handle non-finite values.
Results may differ from a plain program's by a relative error of at most 0.02.
Values may be sent and summed in bfloat16 or wider, within the bound.
A program may use at most 64 MiB of HBM per device.

v0:
```python
import jax
import jax.numpy as jnp
from jax import lax
from jax.sharding import PartitionSpec as P

DMAX = 64


def with_halo(x, sides, width):
    for axis, dim in sides:
        devices, length = (lax.axis_size(axis), x.shape[dim])
        up = [(i, (i + 1) % devices) for i in range(devices - 1)]
        down = [(j, i) for i, j in up]
        last = lax.slice_in_dim(x, length - width, length, axis=dim)
        leading = lax.slice_in_dim(x, 0, width, axis=dim)
        before = lax.ppermute(last, axis, up)
        after = lax.ppermute(leading, axis, down)
        x = jnp.concatenate([before, x, after], axis=dim)
    return x


def passed_along(block, axis, distance):
    devices = range(lax.axis_size(axis))
    route = [(i - distance, i) for i in devices if i - distance in devices]
    return lax.ppermute(block, axis, route)


def activate(values):
    normed = values * lax.rsqrt(jnp.mean(values * values, axis=-1, keepdims=True) + 1e-06)
    return jax.nn.gelu(normed, approximate=True)


def shards(inputs, cotangent, weights, tap_weights, projection, dilations):
    segment_index = lax.axis_index("segment")
    width = inputs.shape[2]
    pair_weights, pair_taps, pair_tests = (weights, tap_weights, projection)
    rows_in = inputs[0]
    grad_out = cotangent[0]
    own_dilation = jnp.where(segment_index == 0, dilations[0], dilations[1])
    late_index = 0
    length = rows_in.shape[0]

    def act_rims(values):
        return with_halo(values, (("ctx", 0),), DMAX)

    def grad_rims(values):
        return with_halo(values, (("ctx", 0),), DMAX)

    full_weights = lax.all_gather(pair_weights, "ctx", axis=1, tiled=True)

    def backward_product(grad, which):
        return lax.dot_general(
            grad, full_weights[which], (((1,), (1,)), ((), ())), preferred_element_type=jnp.float32
        )

    def mix(rows, which, dilation):
        taps = pair_taps[which]
        lower = DMAX - dilation
        upper = DMAX + dilation
        activated = activate(rows.astype(jnp.float32)).astype(jnp.bfloat16)
        padded = act_rims(activated)
        before = lax.dynamic_slice_in_dim(padded, lower, length, 0)
        after = lax.dynamic_slice_in_dim(padded, upper, length, 0)
        mixed = taps[0] * before + taps[1] * activated + taps[2] * after
        return mixed.astype(jnp.bfloat16)

    def backward(rows, mixed, grad, which, dilation):
        taps = pair_taps[which]
        lower = DMAX - dilation
        upper = DMAX + dilation
        grad_mixed = backward_product(grad, which).astype(jnp.bfloat16)
        padded = grad_rims(grad_mixed)
        ahead = lax.dynamic_slice_in_dim(padded, upper, length, 0)
        behind = lax.dynamic_slice_in_dim(padded, lower, length, 0)
        grad_act = taps[0] * ahead + taps[1] * grad_mixed + taps[2] * behind
        primal, pullback = jax.vjp(activate, rows.astype(jnp.float32))
        grad_rows = pullback(grad_act)[0]
        grad_in = (grad.astype(jnp.float32) + grad_rows).astype(jnp.bfloat16)
        sketched = jnp.dot(grad, pair_tests[which], preferred_element_type=jnp.float32).astype(
            jnp.bfloat16
        )
        sketch = lax.dot_general(
            sketched, mixed, (((0,), (0,)), ((), ())), preferred_element_type=jnp.float32
        )
        return (grad_in, sketch)

    first_mixed = mix(rows_in, 0, own_dilation)
    section_out = (
        rows_in.astype(jnp.float32)
        + jnp.dot(first_mixed, full_weights[0], preferred_element_type=jnp.float32)
    ).astype(jnp.bfloat16)
    half = width // 2
    received = passed_along(section_out, "segment", 1)
    late_mixed = mix(received, late_index, own_dilation)
    grad_late, sketch_late = backward(received, late_mixed, grad_out, late_index, own_dilation)
    grad_back = passed_along(grad_late, "segment", -1)
    grad_early, sketch_early = backward(rows_in, first_mixed, grad_back, 0, own_dilation)
    local_sketch = jnp.where(segment_index == 1, sketch_late, sketch_early)
    moved = passed_along(grad_early[:, half:], "segment", 1)
    grad_half = jnp.where(segment_index == 0, grad_early[:, :half], moved)
    summed = lax.psum_scatter(
        local_sketch.astype(jnp.bfloat16), "ctx", scatter_dimension=0, tiled=True
    )
    merged = lax.psum(summed, "dp").astype(jnp.float32)
    return (grad_half[None], merged[None])


def solution(mesh):
    in_specs = (
        P("dp", "ctx", None),
        P("dp", "ctx", None),
        P("segment", "ctx", None),
        P("segment", None, None),
        P("segment", None, None),
        P(),
    )
    out_specs = (P("dp", "ctx", "segment"), P("segment", "ctx", None))
    return jax.shard_map(shards, mesh=mesh, in_specs=in_specs, out_specs=out_specs, check_vma=False)
```

profile of v0, /device:TPU:0, one launch (start us, length us, event | category | flops | bytes accessed | tf_op | source)
XLA Modules:
  0.0 245.8 jit_solution(9777423108458225322)
XLA Ops:
  8.0 1.4 fusion.52
  10.6 4.9 %collective-permute-start.2 = (bf16[64,1536]{1,0:T(8,128)(2,1)S(1)}, bf16[64,1536]{1,0:T(8,128)(2,1)S(1)}, u32[]{:S(2)}, u32[]{:S(2)}) collective-permute-start(bf16[64,1536]{1,0:T(8,128)(2,1)S(1)} %get-tuple-element.16), channel_id=1, source_target_pairs={{0,2},{2,4},{4,6},{6,8},{8,10},{10,12},{12,14},{1,3},{3,5},{5,7},{... | collective-permute-start | bytes 589832 | tf_op jit(solution)/shard_map/ppermute | solution.py:16
  15.5 1.3 collective-permute-start.3
  19.8 4.1 %collective-permute-done.3 = bf16[64,1536]{1,0:T(8,128)(2,1)S(1)} collective-permute-done((bf16[64,1536]{1,0:T(8,128)(2,1)S(1)}, bf16[64,1536]{1,0:T(8,128)(2,1)S(1)}, u32[]{:S(2)}, u32[]{:S(2)}) %collective-permute-start.3) | collective-permute-done | bytes 196640 | tf_op jit(solution)/shard_map/ppermute | solution.py:17
  24.0 1.2 add_convert_fusion.1
  25.2 67.2 %all-gather.2.cloned.1.call-done = bf16[1,1536,1536]{2,1,0:T(8,128)(2,1)} async-done(((bf16[1,192,1536]{2,1,0:T(8,128)(2,1)}), bf16[1,1536,1536]{2,1,0:T(8,128)(2,1)}) %all-gather.2.cloned.1.call-update) | async-done | bytes 4718608 | tf_op jit(solution)/shard_map/all_gather | solution.py:49
  92.4 3.9 %fusion.19 = bf16[256,1536]{1,0:T(8,128)(2,1)S(1)} fusion(bf16[256,1536]{1,0:T(8,128)(2,1)S(1)} %add_convert_fusion.1, bf16[1,1536,1536]{2,1,0:T(8,128)(2,1)} %all-gather.2.cloned.1.call-done, bf16[1,256,1536]{2,1,0:T(8,128)(2,1)S(1)} %copy-done.1), kind=kOutput, calls=%fused_computation.27 | convolution fusion | flops 1209139200 | bytes 7077888 | tf_op jit(solution)/shard_map/dot_general | solution.py:90
  96.2 1.3 collective-permute-start.4
  97.6 1.4 fusion.22
  99.1 2.5 %collective-permute-start = (bf16[64,1536]{1,0:T(8,128)(2,1)S(1)}, bf16[64,1536]{1,0:T(8,128)(2,1)S(1)}, u32[]{:S(2)}, u32[]{:S(2)}) collective-permute-start(bf16[64,1536]{1,0:T(8,128)(2,1)S(1)} %get-tuple-element.14), channel_id=1, source_target_pairs={{0,2},{2,4},{4,6},{6,8},{8,10},{10,12},{12,14},{1,3},{3,5},{5,7},{... | collective-permute-start | bytes 589832 | tf_op jit(solution)/shard_map/ppermute | solution.py:16
  101.5 1.3 collective-permute-start.1
  102.8 4.0 %collective-permute-done = bf16[64,1536]{1,0:T(8,128)(2,1)S(1)} collective-permute-done((bf16[64,1536]{1,0:T(8,128)(2,1)S(1)}, bf16[64,1536]{1,0:T(8,128)(2,1)S(1)}, u32[]{:S(2)}, u32[]{:S(2)}) %collective-permute-start) | collective-permute-done | bytes 196640 | tf_op jit(solution)/shard_map/ppermute | solution.py:16
  106.8 2.3 collective-permute-done.1
  109.5 2.5 %fusion.45 = (f32[256]{0:T(256)S(1)}, f32[256,1536]{1,0:T(8,128)S(1)}, bf16[256,1536]{1,0:T(8,128)(2,1)S(1)}) fusion(bf16[256,1536]{1,0:T(8,128)(2,1)S(1)} %collective-permute-done.4, f32[256]{0:T(256)S(1)} %fusion.70, bf16[384,1536]{1,0:T(8,128)(2,1)S(1)} %pad_maximum_fusion, s32[]{:T(128)S(6)} %select_n.35, f32[1536]{0:T(1024)S(1)} %get-tuple-element.3, ...), kind=kLoop, calls=%fused_computation.49 | loop fusion | flops 12975872 | bytes 5525512 | tf_op jit(solution)/shard_map/transpose(jvp())/reduce_sum | solution.py:29
  112.0 1.4 fusion.35
  113.3 1.3 collective-permute-start.5
  115.4 4.6 %collective-permute-start.9 = (bf16[64,1536]{1,0:T(8,128)(2,1)}, bf16[64,1536]{1,0:T(8,128)(2,1)S(1)}, u32[]{:S(2)}, u32[]{:S(2)}) collective-permute-start(bf16[64,1536]{1,0:T(8,128)(2,1)} %get-tuple-element.10), channel_id=1, source_target_pairs={{0,2},{2,4},{4,6},{6,8},{8,10},{10,12},{12,14},{1,3},{3,5},{5,7},{... | collective-permute-start | bytes 589832 | tf_op jit(solution)/shard_map/ppermute | solution.py:16
  120.0 1.3 collective-permute-start.10
  121.3 4.1 %collective-permute-done.9 = bf16[64,1536]{1,0:T(8,128)(2,1)S(1)} collective-permute-done((bf16[64,1536]{1,0:T(8,128)(2,1)}, bf16[64,1536]{1,0:T(8,128)(2,1)S(1)}, u32[]{:S(2)}, u32[]{:S(2)}) %collective-permute-start.9) | collective-permute-done | bytes 196640 | tf_op jit(solution)/shard_map/ppermute | solution.py:16
  125.4 4.4 %collective-permute-done.10 = bf16[64,1536]{1,0:T(8,128)(2,1)S(1)} collective-permute-done((bf16[64,1536]{1,0:T(8,128)(2,1)}, bf16[64,1536]{1,0:T(8,128)(2,1)S(1)}, u32[]{:S(2)}, u32[]{:S(2)}) %collective-permute-start.10) | collective-permute-done | bytes 196640 | tf_op jit(solution)/shard_map/ppermute | solution.py:17
  129.8 1.1 pad_maximum_fusion.3
  130.9 3.9 %fusion.54 = bf16[256,1536]{1,0:T(8,128)(2,1)} fusion(bf16[256,1536]{1,0:T(8,128)(2,1)S(1)} %get-tuple-element.9, bf16[1,1536,256]{2,1,0:T(8,128)(2,1)S(1)} %copy-done, bf16[1,256,1536]{2,1,0:T(8,128)(2,1)} %param.7, bf16[384,1536]{1,0:T(8,128)(2,1)} %pad_maximum_fusion.3, s32[]{:T(128)S(6)} %select_n.34, s32[]{:T(128)S(6)} %select_n.35, ...), kind=kOutput, calls=%fused_computation.66 | convolution fusion | flops 406257664 | bytes 4739080 | tf_op jit(solution)/shard_map/dot_general | solution.py:82
  134.8 3.7 %fusion.25 = bf16[256,1536]{1,0:T(8,128)(2,1)S(1)} fusion(bf16[256,1536]{1,0:T(8,128)(2,1)S(1)} %collective-permute-done.5, bf16[1,1536,1536]{2,1,0:T(8,128)(2,1)} %all-gather.2.cloned.1.call-done), kind=kOutput, calls=%fused_computation.29 | convolution fusion | flops 1208352768 | bytes 6291456 | tf_op jit(solution)/shard_map/dot_general | solution.py:52
  139.4 4.7 %collective-permute-start.6 = (bf16[64,1536]{1,0:T(8,128)(2,1)}, bf16[64,1536]{1,0:T(8,128)(2,1)S(1)}, u32[]{:S(2)}, u32[]{:S(2)}) collective-permute-start(bf16[64,1536]{1,0:T(8,128)(2,1)} %get-tuple-element.12), channel_id=1, source_target_pairs={{0,2},{2,4},{4,6},{6,8},{8,10},{10,12},{12,14},{1,3},{3,5},{5,7},{... | collective-permute-start | bytes 589832 | tf_op jit(solution)/shard_map/ppermute | solution.py:16
  144.1 1.3 collective-permute-start.7
  145.4 3.2 %fusion.18 = bf16[256,1536]{1,0:T(8,128)(2,1)} fusion(bf16[256,1536]{1,0:T(8,128)(2,1)} %fusion.54, bf16[256,1536]{1,0:T(8,128)(2,1)} %copy-done.2, bf16[256,1536]{1,0:T(8,128)(2,1)S(1)} %collective-permute-done.5, bf16[1,1536,256]{2,1,0:T(8,128)(2,1)S(1)} %copy-done, pred[]{:T(512)S(6)} %eq.8), kind=kOutput, calls=%fused_computation.26 | convolution fusion | flops 403111936 | bytes 3932161 | tf_op jit(solution)/shard_map/dot_general | solution.py:82
  148.8 4.6 %collective-permute-done.7 = bf16[64,1536]{1,0:T(8,128)(2,1)S(1)} collective-permute-done((bf16[64,1536]{1,0:T(8,128)(2,1)}, bf16[64,1536]{1,0:T(8,128)(2,1)S(1)}, u32[]{:S(2)}, u32[]{:S(2)}) %collective-permute-start.7) | collective-permute-done | bytes 196640 | tf_op jit(solution)/shard_map/ppermute | solution.py:17
  153.6 2.4 fusion.53
  156.4 1.3 collective-permute-start.8
  157.8 57.4 %reduce-scatter.2.cloned.1.call-done = bf16[32,1536]{1,0:T(8,128)(2,1)} async-done(((bf16[256,1536]{1,0:T(8,128)(2,1)}), bf16[32,1536]{1,0:T(8,128)(2,1)}) %reduce-scatter.2.cloned.1.call-update) | async-done | bytes 98320 | tf_op jit(solution)/shard_map/reduce_scatter | solution.py:101
  216.0 21.7 %all-reduce.2.cloned.1.call-done = bf16[1,32,1536]{2,1,0:T(8,128)(2,1)} async-done(((bf16[1,32,1536]{2,1,0:T(8,128)(2,1)}), bf16[1,32,1536]{2,1,0:T(8,128)(2,1)}) %all-reduce.2.cloned.1.call-update) | async-done | bytes 98320 | tf_op jit(solution)/shard_map/psum | solution.py:104
  237.7 1.6 broadcast_in_dim.23
  (57 shorter events, 7.2 us)
Async XLA Ops:
  7.2 123.8 %copy-start = (bf16[1,1536,256]{2,1,0:T(8,128)(2,1)S(1)}, bf16[1,1536,256]{2,1,0:T(8,128)(2,1)}, u32[]{:S(2)}) copy-start(bf16[1,1536,256]{2,1,0:T(8,128)(2,1)} %param.10) | copy-start | bytes 2359300
  7.2 2.8 %copy-start.1 = (bf16[1,256,1536]{2,1,0:T(8,128)(2,1)S(1)}, bf16[1,256,1536]{2,1,0:T(8,128)(2,1)}, u32[]{:S(2)}) copy-start(bf16[1,256,1536]{2,1,0:T(8,128)(2,1)} %param.6) | copy-start | bytes 2359300
  7.2 85.2 %all-gather.2.cloned.1.call-start = ((), (), s32[]{:S(2)}) async-start(), calls=%async_computation.1 | async-start | bytes 5308416 | tf_op jit(solution)/shard_map/all_gather | solution.py:49
  7.9 8.9 %copy-start.12 = (s32[2]{0:T(128)S(1)}, s32[2]{0:T(128)}, u32[]{:S(2)}) copy-start(s32[2]{0:T(128)} %param.11) | copy-start | bytes 28
  7.9 10.8 %copy-start.9 = (f32[1,3,1536]{2,0,1:T(1,128)S(1)}, f32[1,3,1536]{2,0,1:T(1,128)}, u32[]{:S(2)}) copy-start(f32[1,3,1536]{2,0,1:T(1,128)} %param.9) | copy-start | bytes 55300
  7.9 207.2 %reduce-scatter.2.cloned.1.call-start = ((), (), s32[]{:S(2)}) async-start(), calls=%async_computation.2 | async-start | bytes 884736 | tf_op jit(solution)/shard_map/reduce_scatter | solution.py:101
  9.4 0.6 copy-start.10
  9.9 14.0 %copy-start.7 = (f32[256]{0:T(256)}, f32[256]{0:T(256)S(1)}, u32[]{:S(2)}) copy-start(f32[256]{0:T(256)S(1)} %fusion.69) | copy-start | bytes 3076
  10.6 9.1 %collective-permute-start.2 = (bf16[64,1536]{1,0:T(8,128)(2,1)S(1)}, bf16[64,1536]{1,0:T(8,128)(2,1)S(1)}, u32[]{:S(2)}, u32[]{:S(2)}) collective-permute-start(bf16[64,1536]{1,0:T(8,128)(2,1)S(1)} %get-tuple-element.16), channel_id=1, source_target_pairs={{0,2},{2,4},{4,6},{6,8},{8,10},{10,12},{12,14},{1,3},{3,5},{5,7},{... | collective-permute-start | bytes 589832 | tf_op jit(solution)/shard_map/ppermute | solution.py:16
  15.5 8.3 %collective-permute-start.3 = (bf16[64,1536]{1,0:T(8,128)(2,1)S(1)}, bf16[64,1536]{1,0:T(8,128)(2,1)S(1)}, u32[]{:S(2)}, u32[]{:S(2)}) collective-permute-start(bf16[64,1536]{1,0:T(8,128)(2,1)S(1)} %get-tuple-element.17), channel_id=1, source_target_pairs={{2,0},{4,2},{6,4},{8,6},{10,8},{12,10},{14,12},{3,1},{5,3},{7,5},{... | collective-permute-start | bytes 589832 | tf_op jit(solution)/shard_map/ppermute | solution.py:17
  18.8 90.6 %copy-start.5 = (f32[1536]{0:T(1024)}, f32[1536]{0:T(1024)S(1)}, u32[]{:S(2)}) copy-start(f32[1536]{0:T(1024)S(1)} %get-tuple-element.4) | copy-start | bytes 18436
  25.2 71.1 %copy-start.2 = (bf16[256,1536]{1,0:T(8,128)(2,1)}, bf16[256,1536]{1,0:T(8,128)(2,1)S(1)}, u32[]{:S(2)}) copy-start(bf16[256,1536]{1,0:T(8,128)(2,1)S(1)} %add_convert_fusion.1) | copy-start | bytes 2359300
  25.2 72.4 %copy-start.3 = (bf16[1,256,1536]{2,1,0:T(8,128)(2,1)S(1)}, bf16[1,256,1536]{2,1,0:T(8,128)(2,1)}, u32[]{:S(2)}) copy-start(bf16[1,256,1536]{2,1,0:T(8,128)(2,1)} %param.7) | copy-start | bytes 2359300
  92.4 5.2 %copy-start.13 = (bf16[1,1536,1536]{2,1,0:T(8,128)(2,1)S(1)}, bf16[1,1536,1536]{2,1,0:T(8,128)(2,1)}, u32[]{:S(2)}) copy-start(bf16[1,1536,1536]{2,1,0:T(8,128)(2,1)} %all-gather.2.cloned.1.call-done) | copy-start | bytes 14155780
  96.2 13.0 %collective-permute-start.4 = (bf16[256,1536]{1,0:T(8,128)(2,1)S(1)}, bf16[256,1536]{1,0:T(8,128)(2,1)S(1)}, u32[]{:S(2)}, u32[]{:S(2)}) collective-permute-start(bf16[256,1536]{1,0:T(8,128)(2,1)S(1)} %fusion.19), channel_id=1, source_target_pairs={{0,1},{2,3},{4,5},{6,7},{8,9},{10,11},{12,13},{14,15},{16,17},{18,... | collective-permute-start | bytes 2359304 | tf_op jit(solution)/shard_map/ppermute | solution.py:25
  99.1 7.8 %collective-permute-start = (bf16[64,1536]{1,0:T(8,128)(2,1)S(1)}, bf16[64,1536]{1,0:T(8,128)(2,1)S(1)}, u32[]{:S(2)}, u32[]{:S(2)}) collective-permute-start(bf16[64,1536]{1,0:T(8,128)(2,1)S(1)} %get-tuple-element.14), channel_id=1, source_target_pairs={{0,2},{2,4},{4,6},{6,8},{8,10},{10,12},{12,14},{1,3},{3,5},{5,7},{... | collective-permute-start | bytes 589832 | tf_op jit(solution)/shard_map/ppermute | solution.py:16
  101.5 7.6 %collective-permute-start.1 = (bf16[64,1536]{1,0:T(8,128)(2,1)S(1)}, bf16[64,1536]{1,0:T(8,128)(2,1)S(1)}, u32[]{:S(2)}, u32[]{:S(2)}) collective-permute-start(bf16[64,1536]{1,0:T(8,128)(2,1)S(1)} %get-tuple-element.15), channel_id=1, source_target_pairs={{2,0},{4,2},{6,4},{8,6},{10,8},{12,10},{14,12},{3,1},{5,3},{7,5},{... | collective-permute-start | bytes 589832 | tf_op jit(solution)/shard_map/ppermute | solution.py:17
  109.5 2.5 %copy-start.4 = (bf16[1,256,1536]{2,1,0:T(8,128)(2,1)S(1)}, bf16[1,256,1536]{2,1,0:T(8,128)(2,1)}, u32[]{:S(2)}) copy-start(bf16[1,256,1536]{2,1,0:T(8,128)(2,1)} %param.7) | copy-start | bytes 2359300
  113.3 21.5 %collective-permute-start.5 = (bf16[256,1536]{1,0:T(8,128)(2,1)}, bf16[256,1536]{1,0:T(8,128)(2,1)S(1)}, u32[]{:S(2)}, u32[]{:S(2)}) collective-permute-start(bf16[256,1536]{1,0:T(8,128)(2,1)} %fusion.35), channel_id=1, source_target_pairs={{1,0},{3,2},{5,4},{7,6},{9,8},{11,10},{13,12},{15,14},{17,16},{19,... | collective-permute-start | bytes 2359304 | tf_op jit(solution)/shard_map/ppermute | solution.py:25
  115.4 10.0 %collective-permute-start.9 = (bf16[64,1536]{1,0:T(8,128)(2,1)}, bf16[64,1536]{1,0:T(8,128)(2,1)S(1)}, u32[]{:S(2)}, u32[]{:S(2)}) collective-permute-start(bf16[64,1536]{1,0:T(8,128)(2,1)} %get-tuple-element.10), channel_id=1, source_target_pairs={{0,2},{2,4},{4,6},{6,8},{8,10},{10,12},{12,14},{1,3},{3,5},{5,7},{... | collective-permute-start | bytes 589832 | tf_op jit(solution)/shard_map/ppermute | solution.py:16
  120.0 9.8 %collective-permute-start.10 = (bf16[64,1536]{1,0:T(8,128)(2,1)}, bf16[64,1536]{1,0:T(8,128)(2,1)S(1)}, u32[]{:S(2)}, u32[]{:S(2)}) collective-permute-start(bf16[64,1536]{1,0:T(8,128)(2,1)} %get-tuple-element.11), channel_id=1, source_target_pairs={{2,0},{4,2},{6,4},{8,6},{10,8},{12,10},{14,12},{3,1},{5,3},{7,5},{... | collective-permute-start | bytes 589832 | tf_op jit(solution)/shard_map/ppermute | solution.py:17
  139.4 9.5 %collective-permute-start.6 = (bf16[64,1536]{1,0:T(8,128)(2,1)}, bf16[64,1536]{1,0:T(8,128)(2,1)S(1)}, u32[]{:S(2)}, u32[]{:S(2)}) collective-permute-start(bf16[64,1536]{1,0:T(8,128)(2,1)} %get-tuple-element.12), channel_id=1, source_target_pairs={{0,2},{2,4},{4,6},{6,8},{8,10},{10,12},{12,14},{1,3},{3,5},{5,7},{... | collective-permute-start | bytes 589832 | tf_op jit(solution)/shard_map/ppermute | solution.py:16
  144.1 9.4 %collective-permute-start.7 = (bf16[64,1536]{1,0:T(8,128)(2,1)}, bf16[64,1536]{1,0:T(8,128)(2,1)S(1)}, u32[]{:S(2)}, u32[]{:S(2)}) collective-permute-start(bf16[64,1536]{1,0:T(8,128)(2,1)} %get-tuple-element.13), channel_id=1, source_target_pairs={{2,0},{4,2},{6,4},{8,6},{10,8},{12,10},{14,12},{3,1},{5,3},{7,5},{... | collective-permute-start | bytes 589832 | tf_op jit(solution)/shard_map/ppermute | solution.py:17
  148.6 89.1 %all-reduce.2.cloned.1.call-start = ((), (), s32[]{:S(2)}) async-start(), calls=%async_computation.3 | async-start | bytes 196608 | tf_op jit(solution)/shard_map/psum | solution.py:104
  148.8 4.7 %copy-start.6 = (f32[1536]{0:T(1024)S(1)}, f32[1536]{0:T(1024)}, u32[]{:S(2)}) copy-start(f32[1536]{0:T(1024)} %copy-done.5) | copy-start | bytes 18436
  148.8 4.7 %copy-start.8 = (f32[256]{0:T(256)S(1)}, f32[256]{0:T(256)}, u32[]{:S(2)}) copy-start(f32[256]{0:T(256)} %copy-done.7) | copy-start | bytes 3076
  153.5 2.4 copy-start.11
  156.4 58.8 %collective-permute-start.8 = (bf16[256,768]{1,0:T(8,128)(2,1)S(1)}, bf16[256,768]{1,0:T(8,128)(2,1)S(1)}, u32[]{:S(2)}, u32[]{:S(2)}) collective-permute-start(bf16[256,768]{1,0:T(8,128)(2,1)S(1)} %slice.79), channel_id=1, source_target_pairs={{0,1},{2,3},{4,5},{6,7},{8,9},{10,11},{12,13},{14,15},{16,17},{18,... | collective-permute-start | bytes 1179656 | tf_op jit(solution)/shard_map/ppermute | solution.py:25
Sparse Core Ops, SparseCore 0:
  10.2 82.1 all-gather.1
  148.7 66.4 reduce-scatter.1
  217.4 20.2 all-reduce.1
where the time goes:
time: 246 us
  waiting for transfers between devices  171 us (70%)
  starting transfers between devices  26.1 us (11%)
  matrix products  16.1 us (7%)
  between operations  15.4 us (6%)
  other arithmetic  13.9 us (6%)
  local copies, waits for them, and re-layouts  2.89 us (1%)
    all_gather x1, waiting for transfers between devices, shards(): full_weights = lax.all_gather(pair_weights, 'ctx', axis=1, tiled=True)  67.2 us
    reduce_scatter x1, waiting for transfers between devices, shards(): lax.psum_scatter(local_sketch.astype(jnp.bfloat16), 'ctx', scatter_dimens...  57.4 us
    psum x1, waiting for transfers between devices, shards(): merged = lax.psum(summed, 'dp').astype(jnp.float32)  21.7 us
    ppermute x4, starting transfers between devices, with_halo(): before = lax.ppermute(last, axis, up)  16.7 us
    ppermute x4, waiting for transfers between devices, with_halo(): after = lax.ppermute(leading, axis, down)  15.4 us
    ppermute x4, waiting for transfers between devices, with_halo(): before = lax.ppermute(last, axis, up)  8.97 us
    dot_general x2, matrix products, backward(): lax.dot_general(sketched, mixed, (((0,), (0,)), ((), ())), preferred_elem...  7.08 us
    ppermute x4, starting transfers between devices, with_halo(): after = lax.ppermute(leading, axis, down)  5.17 us
  transfers between devices with their start and end apart: 14, of which 10 were waited for; matrix products, arithmetic and copies ran while one was open for 7% of the time, Pallas kernels for 0%

commit v1 on v0

--- a/solution.py
+++ b/solution.py
@@ -101,7 +101,7 @@
     summed = lax.psum_scatter(
         local_sketch.astype(jnp.bfloat16), "ctx", scatter_dimension=0, tiled=True
     )
-    merged = lax.psum(summed, "dp").astype(jnp.float32)
+    merged = jnp.sum(lax.all_gather(summed, "dp"), axis=0).astype(jnp.float32)
     return (grad_half[None], merged[None])
 
 

time: 246 us -> 229 us (0.931)
  waiting for transfers between devices: 171 us -> 149 us
  blocking collectives: 0 us -> 5.48 us
    psum x1 -> x0, waiting for transfers between devices: 21.7 us -> none  [shards(): merged = lax.psum(summed, 'dp').astype(jnp.float32)]
    all_gather x0 -> x1, blocking collectives: none -> 5.48 us  [shards(): merged = jnp.sum(lax.all_gather(summed, 'dp'), axis=0).astype(jnp.float32)]
  transfers between devices with their start and end apart: 14 -> 13, of which waited for: 10 -> 10; matrix products, arithmetic and copies ran while one was open for 7% -> 8% of each run, Pallas kernels for 0% -> 0%
where the time goes in v1:
time: 229 us; the launch traced here: 228 us
  waiting for transfers between devices  149 us (65%)
  starting transfers between devices  26 us (11%)
  matrix products  16.1 us (7%)
  between operations  15.7 us (7%)
  other arithmetic  13.1 us (6%)
  blocking collectives  5.48 us (2%)
  local copies, waits for them, and re-layouts  2.88 us (1%)
    all_gather x1, waiting for transfers between devices, shards(): full_weights = lax.all_gather(pair_weights, 'ctx', axis=1, tiled=True)  67.2 us
    reduce_scatter x1, waiting for transfers between devices, shards(): lax.psum_scatter(local_sketch.astype(jnp.bfloat16), 'ctx', scatter_dimens...  55.5 us
    ppermute x4, starting transfers between devices, with_halo(): before = lax.ppermute(last, axis, up)  16.7 us
    ppermute x4, waiting for transfers between devices, with_halo(): after = lax.ppermute(leading, axis, down)  15.5 us
    ppermute x4, waiting for transfers between devices, with_halo(): before = lax.ppermute(last, axis, up)  8.97 us
    dot_general x2, matrix products, backward(): lax.dot_general(sketched, mixed, (((0,), (0,)), ((), ())), preferred_elem...  7.07 us
    all_gather x1, blocking collectives, shards(): merged = jnp.sum(lax.all_gather(summed, 'dp'), axis=0).astype(jnp.float32)  5.48 us
    ppermute x4, starting transfers between devices, with_halo(): after = lax.ppermute(leading, axis, down)  5.35 us
  transfers between devices with their start and end apart: 13, of which 10 were waited for; matrix products, arithmetic and copies ran while one was open for 8% of the time, Pallas kernels for 0%

profile of v1, /device:TPU:0, one launch (start us, length us, event | category | flops | bytes accessed | tf_op | source)
XLA Modules:
  0.0 228.4 jit_solution(9061317051728726887)
XLA Ops:
  8.0 1.4 fusion.52
  10.6 4.9 %collective-permute-start.2 = (bf16[64,1536]{1,0:T(8,128)(2,1)S(1)}, bf16[64,1536]{1,0:T(8,128)(2,1)S(1)}, u32[]{:S(2)}, u32[]{:S(2)}) collective-permute-start(bf16[64,1536]{1,0:T(8,128)(2,1)S(1)} %get-tuple-element.16), channel_id=1, source_target_pairs={{0,2},{2,4},{4,6},{6,8},{8,10},{10,12},{12,14},{1,3},{3,5},{5,7},{... | collective-permute-start | bytes 589832 | tf_op jit(solution)/shard_map/ppermute | solution.py:16
  15.5 1.3 collective-permute-start.3
  19.7 4.1 %collective-permute-done.3 = bf16[64,1536]{1,0:T(8,128)(2,1)S(1)} collective-permute-done((bf16[64,1536]{1,0:T(8,128)(2,1)S(1)}, bf16[64,1536]{1,0:T(8,128)(2,1)S(1)}, u32[]{:S(2)}, u32[]{:S(2)}) %collective-permute-start.3) | collective-permute-done | bytes 196640 | tf_op jit(solution)/shard_map/ppermute | solution.py:17
  23.9 1.2 add_convert_fusion.1
  25.2 67.2 %all-gather.3.cloned.1.call-done = bf16[1,1536,1536]{2,1,0:T(8,128)(2,1)} async-done(((bf16[1,192,1536]{2,1,0:T(8,128)(2,1)}), bf16[1,1536,1536]{2,1,0:T(8,128)(2,1)}) %all-gather.3.cloned.1.call-update) | async-done | bytes 4718608 | tf_op jit(solution)/shard_map/all_gather | solution.py:49
  92.4 3.9 %fusion.19 = bf16[256,1536]{1,0:T(8,128)(2,1)S(1)} fusion(bf16[256,1536]{1,0:T(8,128)(2,1)S(1)} %add_convert_fusion.1, bf16[1,1536,1536]{2,1,0:T(8,128)(2,1)} %all-gather.3.cloned.1.call-done, bf16[1,256,1536]{2,1,0:T(8,128)(2,1)S(1)} %copy-done.1), kind=kOutput, calls=%fused_computation.27 | convolution fusion | flops 1209139200 | bytes 7077888 | tf_op jit(solution)/shard_map/dot_general | solution.py:90
  96.2 1.3 collective-permute-start.4
  97.6 1.4 fusion.22
  99.1 2.5 %collective-permute-start = (bf16[64,1536]{1,0:T(8,128)(2,1)S(1)}, bf16[64,1536]{1,0:T(8,128)(2,1)S(1)}, u32[]{:S(2)}, u32[]{:S(2)}) collective-permute-start(bf16[64,1536]{1,0:T(8,128)(2,1)S(1)} %get-tuple-element.14), channel_id=1, source_target_pairs={{0,2},{2,4},{4,6},{6,8},{8,10},{10,12},{12,14},{1,3},{3,5},{5,7},{... | collective-permute-start | bytes 589832 | tf_op jit(solution)/shard_map/ppermute | solution.py:16
  101.5 1.3 collective-permute-start.1
  102.8 4.0 %collective-permute-done = bf16[64,1536]{1,0:T(8,128)(2,1)S(1)} collective-permute-done((bf16[64,1536]{1,0:T(8,128)(2,1)S(1)}, bf16[64,1536]{1,0:T(8,128)(2,1)S(1)}, u32[]{:S(2)}, u32[]{:S(2)}) %collective-permute-start) | collective-permute-done | bytes 196640 | tf_op jit(solution)/shard_map/ppermute | solution.py:16
  106.8 2.3 %collective-permute-done.1 = bf16[64,1536]{1,0:T(8,128)(2,1)S(1)} collective-permute-done((bf16[64,1536]{1,0:T(8,128)(2,1)S(1)}, bf16[64,1536]{1,0:T(8,128)(2,1)S(1)}, u32[]{:S(2)}, u32[]{:S(2)}) %collective-permute-start.1) | collective-permute-done | bytes 196640 | tf_op jit(solution)/shard_map/ppermute | solution.py:17
  109.5 2.5 %fusion.45 = (f32[256]{0:T(256)S(1)}, f32[256,1536]{1,0:T(8,128)S(1)}, bf16[256,1536]{1,0:T(8,128)(2,1)S(1)}) fusion(bf16[256,1536]{1,0:T(8,128)(2,1)S(1)} %collective-permute-done.4, f32[256]{0:T(256)S(1)} %fusion.70, bf16[384,1536]{1,0:T(8,128)(2,1)S(1)} %pad_maximum_fusion, s32[]{:T(128)S(6)} %select_n.35, f32[1536]{0:T(1024)S(1)} %get-tuple-element.3, ...), kind=kLoop, calls=%fused_computation.49 | loop fusion | flops 12975872 | bytes 5525512 | tf_op jit(solution)/shard_map/transpose(jvp())/reduce_sum | solution.py:29
  112.0 1.4 fusion.35
  113.3 1.3 collective-permute-start.5
  115.4 4.6 %collective-permute-start.9 = (bf16[64,1536]{1,0:T(8,128)(2,1)}, bf16[64,1536]{1,0:T(8,128)(2,1)S(1)}, u32[]{:S(2)}, u32[]{:S(2)}) collective-permute-start(bf16[64,1536]{1,0:T(8,128)(2,1)} %get-tuple-element.10), channel_id=1, source_target_pairs={{0,2},{2,4},{4,6},{6,8},{8,10},{10,12},{12,14},{1,3},{3,5},{5,7},{... | collective-permute-start | bytes 589832 | tf_op jit(solution)/shard_map/ppermute | solution.py:16
  120.0 1.3 collective-permute-start.10
  121.3 4.1 %collective-permute-done.9 = bf16[64,1536]{1,0:T(8,128)(2,1)S(1)} collective-permute-done((bf16[64,1536]{1,0:T(8,128)(2,1)}, bf16[64,1536]{1,0:T(8,128)(2,1)S(1)}, u32[]{:S(2)}, u32[]{:S(2)}) %collective-permute-start.9) | collective-permute-done | bytes 196640 | tf_op jit(solution)/shard_map/ppermute | solution.py:16
  125.4 4.4 %collective-permute-done.10 = bf16[64,1536]{1,0:T(8,128)(2,1)S(1)} collective-permute-done((bf16[64,1536]{1,0:T(8,128)(2,1)}, bf16[64,1536]{1,0:T(8,128)(2,1)S(1)}, u32[]{:S(2)}, u32[]{:S(2)}) %collective-permute-start.10) | collective-permute-done | bytes 196640 | tf_op jit(solution)/shard_map/ppermute | solution.py:17
  129.8 1.1 pad_maximum_fusion.3
  131.0 3.9 %fusion.54 = bf16[256,1536]{1,0:T(8,128)(2,1)} fusion(bf16[256,1536]{1,0:T(8,128)(2,1)S(1)} %get-tuple-element.9, bf16[1,1536,256]{2,1,0:T(8,128)(2,1)S(1)} %copy-done, bf16[1,256,1536]{2,1,0:T(8,128)(2,1)} %param.7, bf16[384,1536]{1,0:T(8,128)(2,1)} %pad_maximum_fusion.3, s32[]{:T(128)S(6)} %select_n.34, s32[]{:T(128)S(6)} %select_n.35, ...), kind=kOutput, calls=%fused_computation.66 | convolution fusion | flops 406257664 | bytes 4739080 | tf_op jit(solution)/shard_map/dot_general | solution.py:82
  134.9 3.7 %fusion.25 = bf16[256,1536]{1,0:T(8,128)(2,1)S(1)} fusion(bf16[256,1536]{1,0:T(8,128)(2,1)S(1)} %collective-permute-done.5, bf16[1,1536,1536]{2,1,0:T(8,128)(2,1)} %all-gather.3.cloned.1.call-done), kind=kOutput, calls=%fused_computation.29 | convolution fusion | flops 1208352768 | bytes 6291456 | tf_op jit(solution)/shard_map/dot_general | solution.py:52
  139.4 4.7 %collective-permute-start.6 = (bf16[64,1536]{1,0:T(8,128)(2,1)}, bf16[64,1536]{1,0:T(8,128)(2,1)S(1)}, u32[]{:S(2)}, u32[]{:S(2)}) collective-permute-start(bf16[64,1536]{1,0:T(8,128)(2,1)} %get-tuple-element.12), channel_id=1, source_target_pairs={{0,2},{2,4},{4,6},{6,8},{8,10},{10,12},{12,14},{1,3},{3,5},{5,7},{... | collective-permute-start | bytes 589832 | tf_op jit(solution)/shard_map/ppermute | solution.py:16
  144.1 1.5 collective-permute-start.7
  145.6 3.2 %fusion.18 = bf16[256,1536]{1,0:T(8,128)(2,1)} fusion(bf16[256,1536]{1,0:T(8,128)(2,1)} %fusion.54, bf16[256,1536]{1,0:T(8,128)(2,1)} %copy-done.2, bf16[256,1536]{1,0:T(8,128)(2,1)S(1)} %collective-permute-done.5, bf16[1,1536,256]{2,1,0:T(8,128)(2,1)S(1)} %copy-done, pred[]{:T(512)S(6)} %eq.8), kind=kOutput, calls=%fused_computation.26 | convolution fusion | flops 403111936 | bytes 3932161 | tf_op jit(solution)/shard_map/dot_general | solution.py:82
  148.8 4.7 %collective-permute-done.7 = bf16[64,1536]{1,0:T(8,128)(2,1)S(1)} collective-permute-done((bf16[64,1536]{1,0:T(8,128)(2,1)}, bf16[64,1536]{1,0:T(8,128)(2,1)S(1)}, u32[]{:S(2)}, u32[]{:S(2)}) %collective-permute-start.7) | collective-permute-done | bytes 196640 | tf_op jit(solution)/shard_map/ppermute | solution.py:17
  153.6 2.4 %fusion.53 = (f32[256]{0:T(256)S(1)}, f32[256,1536]{1,0:T(8,128)S(1)}) fusion(bf16[1,256,1536]{2,1,0:T(8,128)(2,1)S(1)} %copy-done.1, f32[256]{0:T(256)S(1)} %copy-done.8, bf16[384,1536]{1,0:T(8,128)(2,1)S(1)} %pad_maximum_fusion.2, s32[]{:T(128)S(6)} %select_n.35, f32[1536]{0:T(1024)S(1)} %get-tuple-element.3, bf16[256,1536]{1,0:T(8,128)(2,1)S(1)} %fusion.25, ...), kind=kLoop, calls=%fused_computation.57 | loop fusion | flops 12189440 | bytes 4739080 | tf_op jit(solution)/shard_map/transpose(jvp())/reduce_sum | solution.py:29
  156.5 1.3 collective-permute-start.8
  157.8 1.3 collective-permute-done.8
  159.9 55.5 %reduce-scatter.2.cloned.1.call-done = bf16[32,1536]{1,0:T(8,128)(2,1)} async-done(((bf16[256,1536]{1,0:T(8,128)(2,1)}), bf16[32,1536]{1,0:T(8,128)(2,1)}) %reduce-scatter.2.cloned.1.call-update) | async-done | bytes 98320 | tf_op jit(solution)/shard_map/reduce_scatter | solution.py:101
  215.4 5.5 %all-gather = bf16[64,1536]{1,0:T(8,128)(2,1)S(1)} all-gather(bf16[32,1536]{1,0:T(8,128)(2,1)} %reduce-scatter.2.cloned.1.call-done), channel_id=2, replica_groups=mesh['dp'=2,'ctx'=8,'segment'=2] {'dp'}, dimensions={0}, use_global_device_ids=true | all-gather | bytes 294912 | tf_op jit(solution)/shard_map/all_gather | solution.py:104
  (56 shorter events, 7.7 us)
Async XLA Ops:
  7.2 123.8 %copy-start = (bf16[1,1536,256]{2,1,0:T(8,128)(2,1)S(1)}, bf16[1,1536,256]{2,1,0:T(8,128)(2,1)}, u32[]{:S(2)}) copy-start(bf16[1,1536,256]{2,1,0:T(8,128)(2,1)} %param.10) | copy-start | bytes 2359300
  7.2 2.8 %copy-start.1 = (bf16[1,256,1536]{2,1,0:T(8,128)(2,1)S(1)}, bf16[1,256,1536]{2,1,0:T(8,128)(2,1)}, u32[]{:S(2)}) copy-start(bf16[1,256,1536]{2,1,0:T(8,128)(2,1)} %param.6) | copy-start | bytes 2359300
  7.2 85.2 %all-gather.3.cloned.1.call-start = ((), (), s32[]{:S(2)}) async-start(), calls=%async_computation.1 | async-start | bytes 5308416 | tf_op jit(solution)/shard_map/all_gather | solution.py:49
  7.9 8.9 %copy-start.12 = (s32[2]{0:T(128)S(1)}, s32[2]{0:T(128)}, u32[]{:S(2)}) copy-start(s32[2]{0:T(128)} %param.11) | copy-start | bytes 28
  7.9 10.8 %copy-start.9 = (f32[1,3,1536]{2,0,1:T(1,128)S(1)}, f32[1,3,1536]{2,0,1:T(1,128)}, u32[]{:S(2)}) copy-start(f32[1,3,1536]{2,0,1:T(1,128)} %param.9) | copy-start | bytes 55300
  7.9 207.4 %reduce-scatter.2.cloned.1.call-start = ((), (), s32[]{:S(2)}) async-start(), calls=%async_computation.2 | async-start | bytes 884736 | tf_op jit(solution)/shard_map/reduce_scatter | solution.py:101
  9.4 0.6 copy-start.10
  9.9 14.0 %copy-start.7 = (f32[256]{0:T(256)}, f32[256]{0:T(256)S(1)}, u32[]{:S(2)}) copy-start(f32[256]{0:T(256)S(1)} %fusion.69) | copy-start | bytes 3076
  10.6 9.1 %collective-permute-start.2 = (bf16[64,1536]{1,0:T(8,128)(2,1)S(1)}, bf16[64,1536]{1,0:T(8,128)(2,1)S(1)}, u32[]{:S(2)}, u32[]{:S(2)}) collective-permute-start(bf16[64,1536]{1,0:T(8,128)(2,1)S(1)} %get-tuple-element.16), channel_id=1, source_target_pairs={{0,2},{2,4},{4,6},{6,8},{8,10},{10,12},{12,14},{1,3},{3,5},{5,7},{... | collective-permute-start | bytes 589832 | tf_op jit(solution)/shard_map/ppermute | solution.py:16
  15.5 8.3 %collective-permute-start.3 = (bf16[64,1536]{1,0:T(8,128)(2,1)S(1)}, bf16[64,1536]{1,0:T(8,128)(2,1)S(1)}, u32[]{:S(2)}, u32[]{:S(2)}) collective-permute-start(bf16[64,1536]{1,0:T(8,128)(2,1)S(1)} %get-tuple-element.17), channel_id=1, source_target_pairs={{2,0},{4,2},{6,4},{8,6},{10,8},{12,10},{14,12},{3,1},{5,3},{7,5},{... | collective-permute-start | bytes 589832 | tf_op jit(solution)/shard_map/ppermute | solution.py:17
  18.8 90.6 %copy-start.5 = (f32[1536]{0:T(1024)}, f32[1536]{0:T(1024)S(1)}, u32[]{:S(2)}) copy-start(f32[1536]{0:T(1024)S(1)} %get-tuple-element.4) | copy-start | bytes 18436
  25.1 67.2 %copy-start.2 = (bf16[256,1536]{1,0:T(8,128)(2,1)}, bf16[256,1536]{1,0:T(8,128)(2,1)S(1)}, u32[]{:S(2)}) copy-start(bf16[256,1536]{1,0:T(8,128)(2,1)S(1)} %add_convert_fusion.1) | copy-start | bytes 2359300
  25.2 72.4 %copy-start.3 = (bf16[1,256,1536]{2,1,0:T(8,128)(2,1)S(1)}, bf16[1,256,1536]{2,1,0:T(8,128)(2,1)}, u32[]{:S(2)}) copy-start(bf16[1,256,1536]{2,1,0:T(8,128)(2,1)} %param.7) | copy-start | bytes 2359300
  92.4 5.2 %copy-start.13 = (bf16[1,1536,1536]{2,1,0:T(8,128)(2,1)S(1)}, bf16[1,1536,1536]{2,1,0:T(8,128)(2,1)}, u32[]{:S(2)}) copy-start(bf16[1,1536,1536]{2,1,0:T(8,128)(2,1)} %all-gather.3.cloned.1.call-done) | copy-start | bytes 14155780
  96.2 13.0 %collective-permute-start.4 = (bf16[256,1536]{1,0:T(8,128)(2,1)S(1)}, bf16[256,1536]{1,0:T(8,128)(2,1)S(1)}, u32[]{:S(2)}, u32[]{:S(2)}) collective-permute-start(bf16[256,1536]{1,0:T(8,128)(2,1)S(1)} %fusion.19), channel_id=1, source_target_pairs={{0,1},{2,3},{4,5},{6,7},{8,9},{10,11},{12,13},{14,15},{16,17},{18,... | collective-permute-start | bytes 2359304 | tf_op jit(solution)/shard_map/ppermute | solution.py:25
  99.1 7.7 %collective-permute-start = (bf16[64,1536]{1,0:T(8,128)(2,1)S(1)}, bf16[64,1536]{1,0:T(8,128)(2,1)S(1)}, u32[]{:S(2)}, u32[]{:S(2)}) collective-permute-start(bf16[64,1536]{1,0:T(8,128)(2,1)S(1)} %get-tuple-element.14), channel_id=1, source_target_pairs={{0,2},{2,4},{4,6},{6,8},{8,10},{10,12},{12,14},{1,3},{3,5},{5,7},{... | collective-permute-start | bytes 589832 | tf_op jit(solution)/shard_map/ppermute | solution.py:16
  101.5 7.6 %collective-permute-start.1 = (bf16[64,1536]{1,0:T(8,128)(2,1)S(1)}, bf16[64,1536]{1,0:T(8,128)(2,1)S(1)}, u32[]{:S(2)}, u32[]{:S(2)}) collective-permute-start(bf16[64,1536]{1,0:T(8,128)(2,1)S(1)} %get-tuple-element.15), channel_id=1, source_target_pairs={{2,0},{4,2},{6,4},{8,6},{10,8},{12,10},{14,12},{3,1},{5,3},{7,5},{... | collective-permute-start | bytes 589832 | tf_op jit(solution)/shard_map/ppermute | solution.py:17
  109.4 2.5 %copy-start.4 = (bf16[1,256,1536]{2,1,0:T(8,128)(2,1)S(1)}, bf16[1,256,1536]{2,1,0:T(8,128)(2,1)}, u32[]{:S(2)}) copy-start(bf16[1,256,1536]{2,1,0:T(8,128)(2,1)} %param.7) | copy-start | bytes 2359300
  113.3 21.5 %collective-permute-start.5 = (bf16[256,1536]{1,0:T(8,128)(2,1)}, bf16[256,1536]{1,0:T(8,128)(2,1)S(1)}, u32[]{:S(2)}, u32[]{:S(2)}) collective-permute-start(bf16[256,1536]{1,0:T(8,128)(2,1)} %fusion.35), channel_id=1, source_target_pairs={{1,0},{3,2},{5,4},{7,6},{9,8},{11,10},{13,12},{15,14},{17,16},{19,... | collective-permute-start | bytes 2359304 | tf_op jit(solution)/shard_map/ppermute | solution.py:25
  115.4 10.0 %collective-permute-start.9 = (bf16[64,1536]{1,0:T(8,128)(2,1)}, bf16[64,1536]{1,0:T(8,128)(2,1)S(1)}, u32[]{:S(2)}, u32[]{:S(2)}) collective-permute-start(bf16[64,1536]{1,0:T(8,128)(2,1)} %get-tuple-element.10), channel_id=1, source_target_pairs={{0,2},{2,4},{4,6},{6,8},{8,10},{10,12},{12,14},{1,3},{3,5},{5,7},{... | collective-permute-start | bytes 589832 | tf_op jit(solution)/shard_map/ppermute | solution.py:16
  120.0 9.8 %collective-permute-start.10 = (bf16[64,1536]{1,0:T(8,128)(2,1)}, bf16[64,1536]{1,0:T(8,128)(2,1)S(1)}, u32[]{:S(2)}, u32[]{:S(2)}) collective-permute-start(bf16[64,1536]{1,0:T(8,128)(2,1)} %get-tuple-element.11), channel_id=1, source_target_pairs={{2,0},{4,2},{6,4},{8,6},{10,8},{12,10},{14,12},{3,1},{5,3},{7,5},{... | collective-permute-start | bytes 589832 | tf_op jit(solution)/shard_map/ppermute | solution.py:17
  139.4 9.4 %collective-permute-start.6 = (bf16[64,1536]{1,0:T(8,128)(2,1)}, bf16[64,1536]{1,0:T(8,128)(2,1)S(1)}, u32[]{:S(2)}, u32[]{:S(2)}) collective-permute-start(bf16[64,1536]{1,0:T(8,128)(2,1)} %get-tuple-element.12), channel_id=1, source_target_pairs={{0,2},{2,4},{4,6},{6,8},{8,10},{10,12},{12,14},{1,3},{3,5},{5,7},{... | collective-permute-start | bytes 589832 | tf_op jit(solution)/shard_map/ppermute | solution.py:16
  144.1 9.4 %collective-permute-start.7 = (bf16[64,1536]{1,0:T(8,128)(2,1)}, bf16[64,1536]{1,0:T(8,128)(2,1)S(1)}, u32[]{:S(2)}, u32[]{:S(2)}) collective-permute-start(bf16[64,1536]{1,0:T(8,128)(2,1)} %get-tuple-element.13), channel_id=1, source_target_pairs={{2,0},{4,2},{6,4},{8,6},{10,8},{12,10},{14,12},{3,1},{5,3},{7,5},{... | collective-permute-start | bytes 589832 | tf_op jit(solution)/shard_map/ppermute | solution.py:17
  148.8 4.8 %copy-start.6 = (f32[1536]{0:T(1024)S(1)}, f32[1536]{0:T(1024)}, u32[]{:S(2)}) copy-start(f32[1536]{0:T(1024)} %copy-done.5) | copy-start | bytes 18436
  148.8 4.8 %copy-start.8 = (f32[256]{0:T(256)S(1)}, f32[256]{0:T(256)}, u32[]{:S(2)}) copy-start(f32[256]{0:T(256)} %copy-done.7) | copy-start | bytes 3076
  153.6 2.4 %copy-start.11 = (f32[256]{0:T(256)S(1)}, f32[256]{0:T(256)}, u32[]{:S(2)}) copy-start(f32[256]{0:T(256)} %copy-done.10) | copy-start | bytes 3076
  156.5 2.6 %collective-permute-start.8 = (bf16[256,768]{1,0:T(8,128)(2,1)S(1)}, bf16[256,768]{1,0:T(8,128)(2,1)S(1)}, u32[]{:S(2)}, u32[]{:S(2)}) collective-permute-start(bf16[256,768]{1,0:T(8,128)(2,1)S(1)} %slice.79), channel_id=1, source_target_pairs={{0,1},{2,3},{4,5},{6,7},{8,9},{10,11},{12,13},{14,15},{16,17},{18,... | collective-permute-start | bytes 1179656 | tf_op jit(solution)/shard_map/ppermute | solution.py:25
Sparse Core Ops, SparseCore 0:
  10.2 82.1 all-gather.2
  148.9 66.4 reduce-scatter.1
